TPU v7x, 256 devices: a whole 4x4x8 slice. The times are simulated.
256 devices in a mesh: seq: 32 (over z, y), mp: 8 (over x, core).
Axes of the slice: x: 4, y: 4, z: 8, core: 2. Of those that a mesh axis runs over, the one named last changes fastest.
Arguments:
- tokens: bfloat16 [12288, 4096], P('seq', 'mp'), may hold values from -6 to 6
- norm_gain: float32 [2, 4096], replicated, may hold values from 0.25 to 1.75
- in_weight: bfloat16 [2, 3, 4096, 4096], P(None, None, 'seq', 'mp'), may hold values from -0.09375 to 0.09375
- feat_filter: float32 [2, 3, 3, 4096], P(None, None, None, 'mp'), may hold values from -3 to 3
- short_filter: float32 [256, 7], P('mp'), may hold values from -3 to 3
- medium_filter: float32 [256, 128], P('mp'), may hold values from -0.4 to 0.4
- out_weight: bfloat16 [4096, 4096], P('seq', 'mp'), may hold values from -0.09375 to 0.09375
Outputs:
- stream: bfloat16 [12288, 4096], P('seq', 'mp')
- mixed: bfloat16 [12288, 4096], P('seq', 'mp')
All inputs are finite; a program needn't handle non-finite values.
Results may differ from a plain program's by a relative error of at most 0.015.
Values may be sent and summed in bfloat16 or wider, within the bound.
A program may use at most 128 MiB of HBM per device.

v0:
```python
import jax
import jax.numpy as jnp
from jax import lax
from jax.sharding import PartitionSpec as P


def shifted(x, axis, by):
    peers = lax.axis_size(axis)
    pairs = [(i, i + by) for i in range(peers) if 0 <= i + by < peers]
    return lax.ppermute(x, axis, pairs)


def causal_taps(extended, taps, count):
    reach = taps.shape[0] - 1
    offset = extended.shape[0] - count - reach
    values = extended.astype(jnp.float32)
    total = jnp.zeros((count, extended.shape[1]), jnp.float32)
    for index in range(reach + 1):
        begin = offset + reach - index
        total = total + taps[index] * values[begin : begin + count]
    return total


def toeplitz_conv(kv_ext, filt, count):
    width = filt.shape[1]
    channels = kv_ext.shape[1]
    groups_here = filt.shape[0]
    per_group = channels // groups_here
    padded = jnp.concatenate([jnp.zeros((1, channels), kv_ext.dtype), kv_ext], axis=0)
    blocks = padded.astype(jnp.float32).reshape(count // width + 1, width, groups_here, per_group)
    lag = jnp.arange(width)[:, None] - jnp.arange(width)[None, :]
    current = jnp.where(lag >= 0, filt[:, jnp.clip(lag, 0, width - 1)], 0.0)
    earlier = jnp.where(lag < 0, filt[:, jnp.clip(lag + width, 0, width - 1)], 0.0)
    out = jnp.einsum("gik,bkgc->bigc", current, blocks[1:], precision=lax.Precision.HIGHEST)
    out = out + jnp.einsum("gik,bkgc->bigc", earlier, blocks[:-1], precision=lax.Precision.HIGHEST)
    return out.reshape(count, channels)


def normalized(stream_loc, gain):
    full = lax.all_gather(stream_loc, "mp", axis=1, tiled=True)
    values = full.astype(jnp.float32)
    mean_sq = jnp.mean(values * values, axis=-1, keepdims=True)
    return (values * lax.rsqrt(mean_sq + 1e-06) * gain).astype(jnp.bfloat16)


def project(normed, weights):
    return jnp.einsum(
        "rd,cdf->crf",
        normed,
        lax.all_gather(weights, "seq", axis=1, tiled=True),
        preferred_element_type=jnp.float32,
    ).astype(jnp.bfloat16)


def gated_mix(proj, feat_taps, inner_fn, span):
    rows = proj.shape[1]
    reach = feat_taps.shape[1] - 1
    rim = shifted(proj[:, rows - reach :, :], "seq", 1)
    extended = jnp.concatenate([rim, proj], axis=1)
    query = causal_taps(extended[0], feat_taps[0], rows)
    key_part = causal_taps(extended[1], feat_taps[1], rows)
    value_part = causal_taps(extended[2], feat_taps[2], rows)
    kv_prod = (key_part * value_part).astype(jnp.bfloat16)
    earlier = shifted(kv_prod[rows - span :], "seq", 1)
    kv_ext = jnp.concatenate([earlier, kv_prod], axis=0)
    inner = inner_fn(kv_ext, rows)
    return (query * inner).astype(jnp.bfloat16)


def local(tokens, norm_gain, in_weight, feat_filter, short_filter, medium_filter, out_weight):
    per_group = tokens.shape[1] // short_filter.shape[0]
    short_taps = jnp.repeat(short_filter.T, per_group, axis=1)

    def short_inner(kv_ext, count):
        return causal_taps(kv_ext, short_taps, count)

    def medium_inner(kv_ext, count):
        return toeplitz_conv(kv_ext, medium_filter, count)

    normed = normalized(tokens, norm_gain[0])
    proj = project(normed, in_weight[0])
    first = gated_mix(proj, feat_filter[0], short_inner, short_filter.shape[1] - 1)
    first_full = lax.all_gather(first, "mp", axis=1, tiled=True)
    delta = jnp.dot(
        first_full,
        lax.all_gather(out_weight, "seq", axis=0, tiled=True),
        preferred_element_type=jnp.float32,
    )
    stream = (tokens.astype(jnp.float32) + delta).astype(jnp.bfloat16)
    normed_next = normalized(stream, norm_gain[1])
    proj_next = project(normed_next, in_weight[1])
    mixed = gated_mix(proj_next, feat_filter[1], medium_inner, medium_filter.shape[1] - 1)
    return (stream, mixed)


def solution(mesh):
    placed = (
        P("seq", "mp"),
        P(),
        P(None, None, "seq", "mp"),
        P(None, None, None, "mp"),
        P("mp", None),
        P("mp", None),
        P("seq", "mp"),
    )
    return jax.shard_map(
        local,
        mesh=mesh,
        in_specs=placed,
        out_specs=(P("seq", "mp"), P("seq", "mp")),
        check_vma=False,
    )
```

profile of v0, /device:TPU:88, one launch (start us, length us, event | category | flops | bytes accessed | tf_op | source)
XLA Modules:
  0.0 597.8 jit_solution(11730328731184018714)
XLA Ops:
  7.9 2.1 fusion.119
  10.8 0.9 fusion.121
  11.7 30.4 %all-gather.9.cloned.1.call-done = bf16[384,4096]{1,0:T(8,128)(2,1)} async-done(((bf16[384,512]{1,0:T(8,128)(2,1)}), bf16[384,4096]{1,0:T(8,128)(2,1)}) %all-gather.9.cloned.1.call-update) | async-done | bytes 3145744 | tf_op jit(solution)/shard_map/all_gather | solution.py:40
  42.1 2.7 fusion.4
  44.9 116.5 %all-gather.17.cloned.1.call-done = bf16[1,3,4096,512]{3,2,1,0:T(8,128)(2,1)} async-done(((bf16[1,3,128,512]{3,2,1,0:T(8,128)(2,1)}), bf16[1,3,4096,512]{3,2,1,0:T(8,128)(2,1)}) %all-gather.17.cloned.1.call-update) | async-done | bytes 12582928 | tf_op jit(solution)/shard_map/all_gather | solution.py:50
  161.4 8.3 %fusion.39 = bf16[3,384,512]{2,1,0:T(8,128)(2,1)S(1)} fusion(bf16[1,3,4096,512]{3,2,1,0:T(8,128)(2,1)} %all-gather.17.cloned.1.call-done, bf16[384,4096]{1,0:T(8,128)(2,1)S(1)} %copy-done.1, f32[4096]{0:T(1024)S(1)} %bitcast.255, f32[384]{0:T(512)S(1)} %add_rsqrt_fusion.1), kind=kOutput, calls=%fused_computation.35 | convolution fusion | flops 4838719488 | bytes 16926208 | tf_op jit(solution)/shard_map/rd,cdf->crf/dot_general | solution.py:47
  169.7 6.5 %collective-permute-start = (bf16[3,2,512]{2,1,0:T(2,128)(2,1)S(1)}, bf16[3,2,512]{2,1,0:T(2,128)(2,1)S(1)}, u32[]{:S(2)}, u32[]{:S(2)}) collective-permute-start(bf16[3,2,512]{2,1,0:T(2,128)(2,1)S(1)} %slice.436), channel_id=1, source_target_pairs={{0,8},{8,16},{16,24},{24,32},{32,40},{40,48},{48,56},{56,64},{64,7... | collective-permute-start | bytes 18440 | tf_op jit(solution)/shard_map/ppermute | solution.py:10
  176.8 0.7 collective-permute-done
  178.3 6.3 %collective-permute-start.1 = (bf16[6,512]{1,0:T(8,128)(2,1)S(1)}, bf16[6,512]{1,0:T(8,128)(2,1)S(1)}, u32[]{:S(2)}, u32[]{:S(2)}) collective-permute-start(bf16[6,512]{1,0:T(8,128)(2,1)S(1)} %slice.450), channel_id=1, source_target_pairs={{0,8},{8,16},{16,24},{24,32},{32,40},{40,48},{48,56},{56,64},{64,7... | collective-permute-start | bytes 18440 | tf_op jit(solution)/shard_map/ppermute | solution.py:10
  186.1 1.7 fusion.76
  187.9 55.7 %all-gather.13.cloned.1.call-done = bf16[4096,512]{1,0:T(8,128)(2,1)} async-done(((bf16[128,512]{1,0:T(8,128)(2,1)}), bf16[4096,512]{1,0:T(8,128)(2,1)}) %all-gather.13.cloned.1.call-update) | async-done | bytes 4194320 | tf_op jit(solution)/shard_map/all_gather | solution.py:86
  243.6 32.9 %all-gather.11.cloned.1.call-done = bf16[384,4096]{1,0:T(8,128)(2,1)} async-done(((bf16[384,512]{1,0:T(8,128)(2,1)}), bf16[384,4096]{1,0:T(8,128)(2,1)}) %all-gather.11.cloned.1.call-update) | async-done | bytes 3145744 | tf_op jit(solution)/shard_map/all_gather | solution.py:83
  276.5 5.7 fusion.50
  282.8 29.9 %all-gather.15.cloned.1.call-done = bf16[384,4096]{1,0:T(8,128)(2,1)} async-done(((bf16[384,512]{1,0:T(8,128)(2,1)}), bf16[384,4096]{1,0:T(8,128)(2,1)}) %all-gather.15.cloned.1.call-update) | async-done | bytes 3145744 | tf_op jit(solution)/shard_map/all_gather | solution.py:40
  312.7 2.7 fusion.7
  315.4 116.4 %all-gather.19.cloned.1.call-done = bf16[1,3,4096,512]{3,2,1,0:T(8,128)(2,1)} async-done(((bf16[1,3,128,512]{3,2,1,0:T(8,128)(2,1)}), bf16[1,3,4096,512]{3,2,1,0:T(8,128)(2,1)}) %all-gather.19.cloned.1.call-update) | async-done | bytes 12582928 | tf_op jit(solution)/shard_map/all_gather | solution.py:50
  431.8 8.2 %fusion.34 = bf16[3,384,512]{2,1,0:T(8,128)(2,1)S(1)} fusion(bf16[1,3,4096,512]{3,2,1,0:T(8,128)(2,1)} %all-gather.19.cloned.1.call-done, bf16[384,4096]{1,0:T(8,128)(2,1)S(1)} %copy-done.2, f32[4096]{0:T(1024)S(1)} %bitcast.254, f32[384]{0:T(512)S(1)} %add_rsqrt_fusion), kind=kOutput, calls=%fused_computation.34 | convolution fusion | flops 4838719488 | bytes 16926208 | tf_op jit(solution)/shard_map/rd,cdf->crf/dot_general | solution.py:47
  440.1 6.5 %collective-permute-start.2 = (bf16[3,2,512]{2,1,0:T(2,128)(2,1)S(1)}, bf16[3,2,512]{2,1,0:T(2,128)(2,1)S(1)}, u32[]{:S(2)}, u32[]{:S(2)}) collective-permute-start(bf16[3,2,512]{2,1,0:T(2,128)(2,1)S(1)} %slice.458), channel_id=1, source_target_pairs={{0,8},{8,16},{16,24},{24,32},{32,40},{40,48},{48,56},{56,64},{64,7... | collective-permute-start | bytes 18440 | tf_op jit(solution)/shard_map/ppermute | solution.py:10
  446.7 1.3 collective-permute-done.2
  448.8 6.5 %collective-permute-start.3 = (bf16[127,512]{1,0:T(8,128)(2,1)S(1)}, bf16[127,512]{1,0:T(8,128)(2,1)}, u32[]{:S(2)}, u32[]{:S(2)}) collective-permute-start(bf16[127,512]{1,0:T(8,128)(2,1)S(1)} %slice.472), channel_id=1, source_target_pairs={{0,8},{8,16},{16,24},{24,32},{32,40},{40,48},{48,56},{56,64},{64,7... | collective-permute-start | bytes 390152 | tf_op jit(solution)/shard_map/ppermute | solution.py:10
  456.0 54.8 %gather_fusion.1 = f32[16384,32]{1,0:T(8,128)} fusion(f32[32,128]{0,1:T(8,128)S(1)} %copy.17, s32[16384]{0:T(1024)S(1)} %fusion.114), kind=kCustom, calls=%fused_computation.1 | custom fusion | bytes 4259840 | tf_op jit(solution)/shard_map/gather | solution.py:33
  510.8 5.5 copy.22
  516.3 54.8 %gather_fusion = f32[16384,32]{1,0:T(8,128)} fusion(f32[32,128]{0,1:T(8,128)S(1)} %copy.17, s32[16384]{0:T(1024)S(1)} %fusion.112), kind=kCustom, calls=%fused_computation | custom fusion | bytes 4259840 | tf_op jit(solution)/shard_map/gather | solution.py:32
  571.1 6.4 %copy.18 = f32[128,128,32]{1,0,2:T(8,128)} copy(f32[128,128,32]{2,1,0:T(8,128)} %bitcast.250) | data formatting | bytes 4194304 | tf_op jit(solution)/shard_map/gather | solution.py:32
  577.5 0.9 copy.16
  578.4 2.0 slice.428
  580.5 1.8 pad_maximum_fusion.2
  582.3 1.2 copy.20
  583.5 0.9 slice.431
  584.4 2.9 fusion.18
  587.4 1.8 fusion.47
  590.0 1.0 fusion.70
  (74 shorter events, 7.5 us)
Async XLA Ops:
  7.2 35.0 %all-gather.9.cloned.1.call-start = ((), (), s32[]{:S(2)}) async-start(), calls=%async_computation | async-start | bytes 3538944 | tf_op jit(solution)/shard_map/all_gather | solution.py:40
  7.9 153.5 %all-gather.17.cloned.1.call-start = ((), (), s32[]{:S(2)}) async-start(), calls=%async_computation.4 | async-start | bytes 12976128 | tf_op jit(solution)/shard_map/all_gather | solution.py:50
  10.0 233.5 %all-gather.13.cloned.1.call-start = ((), (), s32[]{:S(2)}) async-start(), calls=%async_computation.2 | async-start | bytes 4325376 | tf_op jit(solution)/shard_map/all_gather | solution.py:86
  10.8 265.7 %all-gather.11.cloned.1.call-start = ((), (), s32[]{:S(2)}) async-start(), calls=%async_computation.1 | async-start | bytes 3538944 | tf_op jit(solution)/shard_map/all_gather | solution.py:83
  42.1 119.3 %copy-start.1 = (bf16[384,4096]{1,0:T(8,128)(2,1)S(1)}, bf16[384,4096]{1,0:T(8,128)(2,1)}, u32[]{:S(2)}) copy-start(bf16[384,4096]{1,0:T(8,128)(2,1)} %all-gather.9.cloned.1.call-done) | copy-start | bytes 9437188
  161.4 14.8 %copy-start.6 = (f32[2,3,3,512]{3,0,2,1:T(2,128)S(1)}, f32[2,3,3,512]{3,0,2,1:T(2,128)}, u32[]{:S(2)}) copy-start(f32[2,3,3,512]{3,0,2,1:T(2,128)} %param.10) | copy-start | bytes 110596
  169.7 7.8 %collective-permute-start = (bf16[3,2,512]{2,1,0:T(2,128)(2,1)S(1)}, bf16[3,2,512]{2,1,0:T(2,128)(2,1)S(1)}, u32[]{:S(2)}, u32[]{:S(2)}) collective-permute-start(bf16[3,2,512]{2,1,0:T(2,128)(2,1)S(1)} %slice.436), channel_id=1, source_target_pairs={{0,8},{8,16},{16,24},{24,32},{32,40},{40,48},{48,56},{56,64},{64,7... | collective-permute-start | bytes 18440 | tf_op jit(solution)/shard_map/ppermute | solution.py:10
  177.8 6.8 %copy-start.11 = (f32[32,7]{0,1:T(8,128)S(1)}, f32[32,7]{0,1:T(8,128)}, u32[]{:S(2)}) copy-start(f32[32,7]{0,1:T(8,128)} %param.11) | copy-start | bytes 2692
  178.3 7.7 %collective-permute-start.1 = (bf16[6,512]{1,0:T(8,128)(2,1)S(1)}, bf16[6,512]{1,0:T(8,128)(2,1)S(1)}, u32[]{:S(2)}, u32[]{:S(2)}) collective-permute-start(bf16[6,512]{1,0:T(8,128)(2,1)S(1)} %slice.450), channel_id=1, source_target_pairs={{0,8},{8,16},{16,24},{24,32},{32,40},{40,48},{48,56},{56,64},{64,7... | collective-permute-start | bytes 18440 | tf_op jit(solution)/shard_map/ppermute | solution.py:10
  186.1 90.3 %copy-start.4 = (bf16[384,512]{1,0:T(8,128)(2,1)S(1)}, bf16[384,512]{1,0:T(8,128)(2,1)}, u32[]{:S(2)}) copy-start(bf16[384,512]{1,0:T(8,128)(2,1)} %param.7) | copy-start | bytes 1179652
  187.8 124.9 %all-gather.15.cloned.1.call-start = ((), (), s32[]{:S(2)}) async-start(), calls=%async_computation.3 | async-start | bytes 3538944 | tf_op jit(solution)/shard_map/all_gather | solution.py:40
  282.2 149.6 %all-gather.19.cloned.1.call-start = ((), (), s32[]{:S(2)}) async-start(), calls=%async_computation.5 | async-start | bytes 12976128 | tf_op jit(solution)/shard_map/all_gather | solution.py:50
  312.7 119.1 %copy-start.2 = (bf16[384,4096]{1,0:T(8,128)(2,1)S(1)}, bf16[384,4096]{1,0:T(8,128)(2,1)}, u32[]{:S(2)}) copy-start(bf16[384,4096]{1,0:T(8,128)(2,1)} %all-gather.15.cloned.1.call-done) | copy-start | bytes 9437188
  440.1 7.8 %collective-permute-start.2 = (bf16[3,2,512]{2,1,0:T(2,128)(2,1)S(1)}, bf16[3,2,512]{2,1,0:T(2,128)(2,1)S(1)}, u32[]{:S(2)}, u32[]{:S(2)}) collective-permute-start(bf16[3,2,512]{2,1,0:T(2,128)(2,1)S(1)} %slice.458), channel_id=1, source_target_pairs={{0,8},{8,16},{16,24},{24,32},{32,40},{40,48},{48,56},{56,64},{64,7... | collective-permute-start | bytes 18440 | tf_op jit(solution)/shard_map/ppermute | solution.py:10
  448.2 7.7 %copy-start.7 = (f32[32,128]{1,0:T(8,128)S(1)}, f32[32,128]{1,0:T(8,128)}, u32[]{:S(2)}) copy-start(f32[32,128]{1,0:T(8,128)} %param.12) | copy-start | bytes 49156
  448.8 131.7 %collective-permute-start.3 = (bf16[127,512]{1,0:T(8,128)(2,1)S(1)}, bf16[127,512]{1,0:T(8,128)(2,1)}, u32[]{:S(2)}, u32[]{:S(2)}) collective-permute-start(bf16[127,512]{1,0:T(8,128)(2,1)S(1)} %slice.472), channel_id=1, source_target_pairs={{0,8},{8,16},{16,24},{24,32},{32,40},{40,48},{48,56},{56,64},{64,7... | collective-permute-start | bytes 390152 | tf_op jit(solution)/shard_map/ppermute | solution.py:10
  577.5 6.9 %copy-start.5 = (pred[128,128]{1,0:T(8,128)(4,1)S(1)}, pred[128,128]{1,0:T(8,128)(4,1)}, u32[]{:S(2)}) copy-start(pred[128,128]{1,0:T(8,128)(4,1)} %fusion.115) | copy-start | bytes 49156
  584.4 3.0 copy-start
  584.4 3.0 copy-start.3
  589.1 0.8 copy-start.8
  589.1 0.8 copy-start.9
  589.1 0.8 copy-start.10
Sparse Core Ops, SparseCore 0:
  9.8 32.2 all-gather.8
  45.3 116.0 all-gather.16
  164.0 79.5 all-gather.12
  245.8 30.5 all-gather.10
  282.3 30.3 all-gather.14
  315.7 116.0 all-gather.18
where the time goes:
time: 598 us
  waiting for transfers between devices  386 us (65%)
  local copies, waits for them, and re-layouts  132 us (22%)
  matrix products  26.9 us (4%)
  starting transfers between devices  26 us (4%)
  between operations  14.4 us (2%)
  other arithmetic  12.3 us (2%)
    all_gather x2, waiting for transfers between devices, project(): lax.all_gather(weights, 'seq', axis=1, tiled=True)  233 us
    gather x2, local copies, waits for them, and re-layouts, toeplitz_conv(): current = jnp.where(lag >= 0, filt[:, jnp.clip(lag, 0, width - 1)], 0.0)  61.2 us
    all_gather x2, waiting for transfers between devices, normalized(): full = lax.all_gather(stream_loc, 'mp', axis=1, tiled=True)  60.3 us
    gather x2, local copies, waits for them, and re-layouts, toeplitz_conv(): filt[:, jnp.clip(lag + width, 0, width - 1)]  60.3 us
    all_gather x1, waiting for transfers between devices, local(): lax.all_gather(out_weight, 'seq', axis=0, tiled=True)  55.7 us
    all_gather x1, waiting for transfers between devices, local(): first_full = lax.all_gather(first, 'mp', axis=1, tiled=True)  32.9 us
    ppermute x4, starting transfers between devices, shifted(): return lax.ppermute(x, axis, pairs)  25.8 us
    dot_general x2, matrix products, project(): jnp.einsum('rd,cdf->crf', normed, lax.all_gather(weights, 'seq', axis=1,...  16.5 us
  transfers between devices with their start and end apart: 10, of which 9 were waited for; matrix products, arithmetic and copies ran while one was open for 24% of the time, Pallas kernels for 0%

commit v1 on v0

--- a/solution.py
+++ b/solution.py
@@ -83,7 +83,9 @@
     first_full = lax.all_gather(first, "mp", axis=1, tiled=True)
     delta = jnp.dot(
         first_full,
-        lax.all_gather(out_weight, "seq", axis=0, tiled=True),
+        jnp.concatenate(
+            lax.all_to_all(jnp.stack([out_weight] * lax.axis_size("seq")), "seq", 0, 0), axis=0
+        ),
         preferred_element_type=jnp.float32,
     )
     stream = (tokens.astype(jnp.float32) + delta).astype(jnp.bfloat16)

time: 598 us -> 577 us (0.965)
  waiting for transfers between devices: 386 us -> 352 us
  starting transfers between devices: 26 us -> 36.8 us
    all_gather x1 -> x0, waiting for transfers between devices: 55.7 us -> none  [local(): lax.all_gather(out_weight, 'seq', axis=0, tiled=True)]
    all_gather x2, waiting for transfers between devices: 233 us -> 268 us  [project(): lax.all_gather(weights, 'seq', axis=1, tiled=True)]
    all_gather x2, waiting for transfers between devices: 60.3 us -> 47.8 us  [normalized(): full = lax.all_gather(stream_loc, 'mp', axis=1, tiled=True)]
    all_to_all x0 -> x1, starting transfers between devices: none -> 10.8 us  [local(): lax.all_to_all(jnp.stack([out_weight] * lax.axis_size('seq')), 'seq', 0, 0)]
  transfers between devices with their start and end apart: 10 -> 10, of which waited for: 9 -> 8; matrix products, arithmetic and copies ran while one was open for 24% -> 26% of each run, Pallas kernels for 0% -> 0%
where the time goes in v1:
time: 577 us
  waiting for transfers between devices  352 us (61%)
  local copies, waits for them, and re-layouts  135 us (23%)
  starting transfers between devices  36.8 us (6%)
  matrix products  26.9 us (5%)
  between operations  14.1 us (2%)
  other arithmetic  12.3 us (2%)
    all_gather x2, waiting for transfers between devices, project(): lax.all_gather(weights, 'seq', axis=1, tiled=True)  268 us
    gather x2, local copies, waits for them, and re-layouts, toeplitz_conv(): current = jnp.where(lag >= 0, filt[:, jnp.clip(lag, 0, width - 1)], 0.0)  61.2 us
    gather x2, local copies, waits for them, and re-layouts, toeplitz_conv(): filt[:, jnp.clip(lag + width, 0, width - 1)]  60.3 us
    all_gather x2, waiting for transfers between devices, normalized(): full = lax.all_gather(stream_loc, 'mp', axis=1, tiled=True)  47.8 us
    all_gather x1, waiting for transfers between devices, local(): first_full = lax.all_gather(first, 'mp', axis=1, tiled=True)  32.4 us
    ppermute x4, starting transfers between devices, shifted(): return lax.ppermute(x, axis, pairs)  25.8 us
    dot_general x2, matrix products, project(): jnp.einsum('rd,cdf->crf', normed, lax.all_gather(weights, 'seq', axis=1,...  16.5 us
  transfers between devices with their start and end apart: 10, of which 8 were waited for; matrix products, arithmetic and copies ran while one was open for 26% of the time, Pallas kernels for 0%

profile of v1, /device:TPU:88, one launch (start us, length us, event | category | flops | bytes accessed | tf_op | source)
XLA Modules:
  0.0 576.8 jit_solution(15837616374100387295)
XLA Ops:
  7.9 2.1 fusion.119
  10.0 3.3 stack.2
  13.4 10.8 %all-to-all-start = ((bf16[32,128,512]{2,1,0:T(8,128)(2,1)}), bf16[32,128,512]{2,1,0:T(8,128)(2,1)}, u32[]{:S(2)}, u32[]{:S(2)}) async-start(bf16[32,128,512]{2,1,0:T(8,128)(2,1)} %stack.2), calls=%async_computation | async-start | bytes 8388608 | tf_op jit(solution)/shard_map/all_to_all | solution.py:87
  24.2 17.9 %all-gather.8.cloned.1.call-done = bf16[384,4096]{1,0:T(8,128)(2,1)} async-done(((bf16[384,512]{1,0:T(8,128)(2,1)}), bf16[384,4096]{1,0:T(8,128)(2,1)}) %all-gather.8.cloned.1.call-update) | async-done | bytes 3145744 | tf_op jit(solution)/shard_map/all_gather | solution.py:40
  42.1 2.7 fusion.4
  44.9 151.9 %all-gather.14.cloned.1.call-done = bf16[1,3,4096,512]{3,2,1,0:T(8,128)(2,1)} async-done(((bf16[1,3,128,512]{3,2,1,0:T(8,128)(2,1)}), bf16[1,3,4096,512]{3,2,1,0:T(8,128)(2,1)}) %all-gather.14.cloned.1.call-update) | async-done | bytes 12582928 | tf_op jit(solution)/shard_map/all_gather | solution.py:50
  196.8 8.3 %fusion.39 = bf16[3,384,512]{2,1,0:T(8,128)(2,1)S(1)} fusion(bf16[1,3,4096,512]{3,2,1,0:T(8,128)(2,1)} %all-gather.14.cloned.1.call-done, bf16[384,4096]{1,0:T(8,128)(2,1)S(1)} %copy-done.1, f32[4096]{0:T(1024)S(1)} %bitcast.256, f32[384]{0:T(512)S(1)} %add_rsqrt_fusion.1), kind=kOutput, calls=%fused_computation.35 | convolution fusion | flops 4838719488 | bytes 16926208 | tf_op jit(solution)/shard_map/rd,cdf->crf/dot_general | solution.py:47
  205.1 6.5 %collective-permute-start = (bf16[3,2,512]{2,1,0:T(2,128)(2,1)S(1)}, bf16[3,2,512]{2,1,0:T(2,128)(2,1)S(1)}, u32[]{:S(2)}, u32[]{:S(2)}) collective-permute-start(bf16[3,2,512]{2,1,0:T(2,128)(2,1)S(1)} %slice.436), channel_id=1, source_target_pairs={{0,8},{8,16},{16,24},{24,32},{32,40},{40,48},{48,56},{56,64},{64,7... | collective-permute-start | bytes 18440 | tf_op jit(solution)/shard_map/ppermute | solution.py:10
  212.2 0.7 collective-permute-done
  213.7 6.3 %collective-permute-start.1 = (bf16[6,512]{1,0:T(8,128)(2,1)S(1)}, bf16[6,512]{1,0:T(8,128)(2,1)S(1)}, u32[]{:S(2)}, u32[]{:S(2)}) collective-permute-start(bf16[6,512]{1,0:T(8,128)(2,1)S(1)} %slice.450), channel_id=1, source_target_pairs={{0,8},{8,16},{16,24},{24,32},{32,40},{40,48},{48,56},{56,64},{64,7... | collective-permute-start | bytes 18440 | tf_op jit(solution)/shard_map/ppermute | solution.py:10
  221.5 1.7 fusion.76
  223.3 32.4 %all-gather.10.cloned.1.call-done = bf16[384,4096]{1,0:T(8,128)(2,1)} async-done(((bf16[384,512]{1,0:T(8,128)(2,1)}), bf16[384,4096]{1,0:T(8,128)(2,1)}) %all-gather.10.cloned.1.call-update) | async-done | bytes 3145744 | tf_op jit(solution)/shard_map/all_gather | solution.py:83
  255.7 5.7 fusion.50
  262.0 29.9 %all-gather.12.cloned.1.call-done = bf16[384,4096]{1,0:T(8,128)(2,1)} async-done(((bf16[384,512]{1,0:T(8,128)(2,1)}), bf16[384,4096]{1,0:T(8,128)(2,1)}) %all-gather.12.cloned.1.call-update) | async-done | bytes 3145744 | tf_op jit(solution)/shard_map/all_gather | solution.py:40
  291.9 2.7 fusion.7
  294.7 116.4 %all-gather.16.cloned.1.call-done = bf16[1,3,4096,512]{3,2,1,0:T(8,128)(2,1)} async-done(((bf16[1,3,128,512]{3,2,1,0:T(8,128)(2,1)}), bf16[1,3,4096,512]{3,2,1,0:T(8,128)(2,1)}) %all-gather.16.cloned.1.call-update) | async-done | bytes 12582928 | tf_op jit(solution)/shard_map/all_gather | solution.py:50
  411.1 8.2 %fusion.34 = bf16[3,384,512]{2,1,0:T(8,128)(2,1)S(1)} fusion(bf16[1,3,4096,512]{3,2,1,0:T(8,128)(2,1)} %all-gather.16.cloned.1.call-done, bf16[384,4096]{1,0:T(8,128)(2,1)S(1)} %copy-done.2, f32[4096]{0:T(1024)S(1)} %bitcast.255, f32[384]{0:T(512)S(1)} %add_rsqrt_fusion), kind=kOutput, calls=%fused_computation.34 | convolution fusion | flops 4838719488 | bytes 16926208 | tf_op jit(solution)/shard_map/rd,cdf->crf/dot_general | solution.py:47
  419.3 6.5 %collective-permute-start.2 = (bf16[3,2,512]{2,1,0:T(2,128)(2,1)S(1)}, bf16[3,2,512]{2,1,0:T(2,128)(2,1)S(1)}, u32[]{:S(2)}, u32[]{:S(2)}) collective-permute-start(bf16[3,2,512]{2,1,0:T(2,128)(2,1)S(1)} %slice.458), channel_id=1, source_target_pairs={{0,8},{8,16},{16,24},{24,32},{32,40},{40,48},{48,56},{56,64},{64,7... | collective-permute-start | bytes 18440 | tf_op jit(solution)/shard_map/ppermute | solution.py:10
  425.9 1.3 collective-permute-done.2
  428.0 6.5 %collective-permute-start.3 = (bf16[127,512]{1,0:T(8,128)(2,1)S(1)}, bf16[127,512]{1,0:T(8,128)(2,1)}, u32[]{:S(2)}, u32[]{:S(2)}) collective-permute-start(bf16[127,512]{1,0:T(8,128)(2,1)S(1)} %slice.472), channel_id=1, source_target_pairs={{0,8},{8,16},{16,24},{24,32},{32,40},{40,48},{48,56},{56,64},{64,7... | collective-permute-start | bytes 390152 | tf_op jit(solution)/shard_map/ppermute | solution.py:10
  435.2 54.8 %gather_fusion.1 = f32[16384,32]{1,0:T(8,128)} fusion(f32[32,128]{0,1:T(8,128)S(1)} %copy.17, s32[16384]{0:T(1024)S(1)} %fusion.114), kind=kCustom, calls=%fused_computation.1 | custom fusion | bytes 4259840 | tf_op jit(solution)/shard_map/gather | solution.py:33
  490.0 5.5 copy.22
  495.5 54.8 %gather_fusion = f32[16384,32]{1,0:T(8,128)} fusion(f32[32,128]{0,1:T(8,128)S(1)} %copy.17, s32[16384]{0:T(1024)S(1)} %fusion.112), kind=kCustom, calls=%fused_computation | custom fusion | bytes 4259840 | tf_op jit(solution)/shard_map/gather | solution.py:32
  550.3 6.4 %copy.18 = f32[128,128,32]{1,0,2:T(8,128)} copy(f32[128,128,32]{2,1,0:T(8,128)} %bitcast.251) | data formatting | bytes 4194304 | tf_op jit(solution)/shard_map/gather | solution.py:32
  556.8 0.9 copy.16
  557.7 2.0 slice.428
  559.7 1.8 pad_maximum_fusion.2
  561.5 1.2 copy.20
  562.7 0.9 slice.431
  563.7 2.9 fusion.18
  566.6 1.8 fusion.47
  569.2 1.0 fusion.70
  (76 shorter events, 6.8 us)
Async XLA Ops:
  7.2 35.0 %all-gather.8.cloned.1.call-start = ((), (), s32[]{:S(2)}) async-start(), calls=%async_computation.1 | async-start | bytes 3538944 | tf_op jit(solution)/shard_map/all_gather | solution.py:40
  7.9 188.9 %all-gather.14.cloned.1.call-start = ((), (), s32[]{:S(2)}) async-start(), calls=%async_computation.4 | async-start | bytes 12976128 | tf_op jit(solution)/shard_map/all_gather | solution.py:50
  13.4 10.8 %copy-start.7 = (f32[2,4096]{1,0:T(2,128)S(1)}, f32[2,4096]{1,0:T(2,128)}, u32[]{:S(2)}) copy-start(f32[2,4096]{1,0:T(2,128)} %param.8) | copy-start | bytes 98308
  13.4 209.9 %all-to-all-start = ((bf16[32,128,512]{2,1,0:T(8,128)(2,1)}), bf16[32,128,512]{2,1,0:T(8,128)(2,1)}, u32[]{:S(2)}, u32[]{:S(2)}) async-start(bf16[32,128,512]{2,1,0:T(8,128)(2,1)} %stack.2), calls=%async_computation | async-start | bytes 8388608 | tf_op jit(solution)/shard_map/all_to_all | solution.py:87
  24.1 231.6 %all-gather.10.cloned.1.call-start = ((), (), s32[]{:S(2)}) async-start(), calls=%async_computation.2 | async-start | bytes 3538944 | tf_op jit(solution)/shard_map/all_gather | solution.py:83
  42.1 154.7 %copy-start.1 = (bf16[384,4096]{1,0:T(8,128)(2,1)S(1)}, bf16[384,4096]{1,0:T(8,128)(2,1)}, u32[]{:S(2)}) copy-start(bf16[384,4096]{1,0:T(8,128)(2,1)} %all-gather.8.cloned.1.call-done) | copy-start | bytes 9437188
  196.8 14.8 %copy-start.6 = (f32[2,3,3,512]{3,0,2,1:T(2,128)S(1)}, f32[2,3,3,512]{3,0,2,1:T(2,128)}, u32[]{:S(2)}) copy-start(f32[2,3,3,512]{3,0,2,1:T(2,128)} %param.10) | copy-start | bytes 110596
  205.1 7.8 %collective-permute-start = (bf16[3,2,512]{2,1,0:T(2,128)(2,1)S(1)}, bf16[3,2,512]{2,1,0:T(2,128)(2,1)S(1)}, u32[]{:S(2)}, u32[]{:S(2)}) collective-permute-start(bf16[3,2,512]{2,1,0:T(2,128)(2,1)S(1)} %slice.436), channel_id=1, source_target_pairs={{0,8},{8,16},{16,24},{24,32},{32,40},{40,48},{48,56},{56,64},{64,7... | collective-permute-start | bytes 18440 | tf_op jit(solution)/shard_map/ppermute | solution.py:10
  213.2 6.8 %copy-start.12 = (f32[32,7]{0,1:T(8,128)S(1)}, f32[32,7]{0,1:T(8,128)}, u32[]{:S(2)}) copy-start(f32[32,7]{0,1:T(8,128)} %param.11) | copy-start | bytes 2692
  213.7 7.7 %collective-permute-start.1 = (bf16[6,512]{1,0:T(8,128)(2,1)S(1)}, bf16[6,512]{1,0:T(8,128)(2,1)S(1)}, u32[]{:S(2)}, u32[]{:S(2)}) collective-permute-start(bf16[6,512]{1,0:T(8,128)(2,1)S(1)} %slice.450), channel_id=1, source_target_pairs={{0,8},{8,16},{16,24},{24,32},{32,40},{40,48},{48,56},{56,64},{64,7... | collective-permute-start | bytes 18440 | tf_op jit(solution)/shard_map/ppermute | solution.py:10
  221.5 34.2 %copy-start.4 = (bf16[384,512]{1,0:T(8,128)(2,1)S(1)}, bf16[384,512]{1,0:T(8,128)(2,1)}, u32[]{:S(2)}) copy-start(bf16[384,512]{1,0:T(8,128)(2,1)} %param.7) | copy-start | bytes 1179652
  223.2 68.7 %all-gather.12.cloned.1.call-start = ((), (), s32[]{:S(2)}) async-start(), calls=%async_computation.3 | async-start | bytes 3538944 | tf_op jit(solution)/shard_map/all_gather | solution.py:40
  261.4 149.6 %all-gather.16.cloned.1.call-start = ((), (), s32[]{:S(2)}) async-start(), calls=%async_computation.5 | async-start | bytes 12976128 | tf_op jit(solution)/shard_map/all_gather | solution.py:50
  291.9 119.1 %copy-start.2 = (bf16[384,4096]{1,0:T(8,128)(2,1)S(1)}, bf16[384,4096]{1,0:T(8,128)(2,1)}, u32[]{:S(2)}) copy-start(bf16[384,4096]{1,0:T(8,128)(2,1)} %all-gather.12.cloned.1.call-done) | copy-start | bytes 9437188
  419.3 7.8 %collective-permute-start.2 = (bf16[3,2,512]{2,1,0:T(2,128)(2,1)S(1)}, bf16[3,2,512]{2,1,0:T(2,128)(2,1)S(1)}, u32[]{:S(2)}, u32[]{:S(2)}) collective-permute-start(bf16[3,2,512]{2,1,0:T(2,128)(2,1)S(1)} %slice.458), channel_id=1, source_target_pairs={{0,8},{8,16},{16,24},{24,32},{32,40},{40,48},{48,56},{56,64},{64,7... | collective-permute-start | bytes 18440 | tf_op jit(solution)/shard_map/ppermute | solution.py:10
  427.5 7.7 %copy-start.8 = (f32[32,128]{1,0:T(8,128)S(1)}, f32[32,128]{1,0:T(8,128)}, u32[]{:S(2)}) copy-start(f32[32,128]{1,0:T(8,128)} %param.12) | copy-start | bytes 49156
  428.0 131.7 %collective-permute-start.3 = (bf16[127,512]{1,0:T(8,128)(2,1)S(1)}, bf16[127,512]{1,0:T(8,128)(2,1)}, u32[]{:S(2)}, u32[]{:S(2)}) collective-permute-start(bf16[127,512]{1,0:T(8,128)(2,1)S(1)} %slice.472), channel_id=1, source_target_pairs={{0,8},{8,16},{16,24},{24,32},{32,40},{40,48},{48,56},{56,64},{64,7... | collective-permute-start | bytes 390152 | tf_op jit(solution)/shard_map/ppermute | solution.py:10
  556.7 6.9 %copy-start.5 = (pred[128,128]{1,0:T(8,128)(4,1)S(1)}, pred[128,128]{1,0:T(8,128)(4,1)}, u32[]{:S(2)}) copy-start(pred[128,128]{1,0:T(8,128)(4,1)} %fusion.115) | copy-start | bytes 49156
  563.6 3.0 copy-start
  563.6 3.0 copy-start.3
  568.4 0.8 copy-start.9
  568.4 0.8 copy-start.10
  568.4 0.8 copy-start.11
Sparse Core Ops, SparseCore 0:
  9.8 32.2 all-gather.7
  45.3 151.4 all-gather.13
  223.3 32.3 all-gather.9
  261.5 30.3 all-gather.11
  294.9 116.0 all-gather.15
